TPU v7x, 128 devices: a whole 4x4x4 slice. The times are simulated.
128 devices in a mesh: ctx: 32 (over z, x, core), tp: 4 (over y).
Axes of the slice: x: 4, y: 4, z: 4, core: 2. Of those that a mesh axis runs over, the one named last changes fastest.
Arguments:
- tokens: bfloat16 [4096, 4096], P('ctx', 'tp'), may hold values from -6 to 6
- in_weight: bfloat16 [4096, 3, 4096], P('ctx', None, 'tp'), may hold values from -0.09375 to 0.09375
- conv_taps: float32 [3, 3, 4096], P(None, None, 'tp'), may hold values from -2.5 to 2.5
- decay_rate: float32 [16, 4096], P(None, 'tp'), may hold values from 0 to 0.034, as said below
- residue: float32 [16, 4096], P(None, 'tp'), may hold values from -1 to 1
- skip: float32 [4096], P('tp'), may hold values from -1 to 1
Outputs:
- mixed: bfloat16 [4096, 4096], P('ctx', 'tp')
Inputs may be any that keep to these rules, and one draw needn't show every extreme that they name: `decay_rate`: positive decay rates of the poles.
All inputs are finite; a program needn't handle non-finite values.
Results may differ from a plain program's by a relative error of at most 0.0063.
Values may be sent and summed in bfloat16 or wider, within the bound.
A program may use at most 128 MiB of HBM per device.

v0:
```python
import math
import jax
import jax.numpy as jnp
from jax import lax
from jax.sharding import PartitionSpec as P


def passed_along(array, axis, by):
    peers = lax.axis_size(axis)
    pairs = [(i, i + by) for i in range(peers) if 0 <= i + by < peers]
    return lax.ppermute(array, axis, pairs)


def entering(array, axis, combine, identity):
    peers, here = (lax.axis_size(axis), lax.axis_index(axis))
    everything = jax.tree.map(lambda part: lax.all_gather(part, axis), array)
    start = jax.tree.map(
        lambda part, zero: jnp.broadcast_to(jnp.asarray(zero, part.dtype), part.shape),
        array,
        identity,
    )

    def turn(k, before):
        reached = k < here
        new = combine(before, jax.tree.map(lambda part: part[k], everything))
        return jax.tree.map(lambda a, b: jnp.where(reached, a, b), new, before)

    return lax.fori_loop(0, peers, turn, start)


def link(earlier, later):
    return (earlier[0] * later[0], later[0] * earlier[1] + later[1])


def per_device(tokens, in_weight, conv_taps, decay_rate, residue, skip):
    rows = tokens.shape[0]
    chans = in_weight.shape[2]
    whole = lax.all_gather(tokens, "tp", axis=1, tiled=True)
    piece = lax.all_gather(in_weight, "ctx", axis=0, tiled=True)
    sums = tuple(
        (jnp.dot(whole, piece[:, g, :], preferred_element_type=jnp.float32) for g in range(3))
    )
    projected = jnp.stack([total.astype(jnp.bfloat16) for total in sums], axis=0)
    edge_out = passed_along(projected[:, rows - 2 :, :], "ctx", 1)
    extended = jnp.concatenate([edge_out, projected], axis=1)
    values = lax.optimization_barrier(extended).astype(jnp.float32)
    filtered = (
        conv_taps[0][:, None, :] * values[:, 2:, :]
        + conv_taps[1][:, None, :] * values[:, 1:-1, :]
        + conv_taps[2][:, None, :] * values[:, :-2, :]
    )
    query = filtered[0]
    gated = filtered[1] * filtered[2]
    span = math.gcd(rows, 32)
    blocks = rows // span
    offsets = jnp.arange(span, dtype=jnp.float32)
    powers = jnp.exp(-decay_rate[None] * offsets[:, None, None])
    response = jnp.sum(residue[None] * powers, axis=1)
    lags = jnp.arange(span)[:, None] - jnp.arange(span)[None, :]
    toeplitz = jnp.where((lags >= 0)[:, :, None], response[jnp.clip(lags, 0, span - 1)], 0.0)
    blocked = gated.reshape(blocks, span, chans)
    inside = jnp.einsum("tsc,bsc->btc", toeplitz, blocked, precision=lax.Precision.HIGHEST)
    tails = jnp.exp(-decay_rate[None] * (span - 1.0 - offsets)[:, None, None])
    ends = jnp.einsum("spc,bsc->bpc", tails, blocked, precision=lax.Precision.HIGHEST)
    block_decay = jnp.broadcast_to(jnp.exp(-decay_rate * span)[None], ends.shape)
    after = lax.associative_scan(link, (block_decay, ends), axis=0)[1]
    final = after[blocks - 1]
    starts = jnp.concatenate([jnp.zeros_like(after[:1]), after[: blocks - 1]], axis=0)
    segment = jnp.exp(-decay_rate * rows)
    carried = entering(
        (segment, final), "ctx", link, (jnp.ones_like(final), jnp.zeros_like(final))
    )[1]
    block_starts = (span * jnp.arange(blocks, dtype=jnp.float32))[:, None, None]
    begin = starts + jnp.exp(-decay_rate[None] * block_starts) * carried[None]
    leading = residue[None] * jnp.exp(-decay_rate[None] * (offsets + 1.0)[:, None, None])
    convolved = inside + jnp.einsum("tpc,bpc->btc", leading, begin, precision=lax.Precision.HIGHEST)
    convolved = convolved.reshape(rows, chans)
    return (query * (convolved + skip[None, :] * gated)).astype(jnp.bfloat16)


def solution(mesh):
    placed = (
        P("ctx", "tp"),
        P("ctx", None, "tp"),
        P(None, None, "tp"),
        P(None, "tp"),
        P(None, "tp"),
        P("tp"),
    )
    return jax.shard_map(
        per_device, mesh=mesh, in_specs=placed, out_specs=P("ctx", "tp"), check_vma=False
    )
```

profile of v0, /device:TPU:32, one launch (start us, length us, event | category | flops | bytes accessed | tf_op | source)
XLA Modules:
  0.0 293.2 jit_solution(15202066247814389937)
XLA Ops:
  8.1 1.5 multiply_exponential_fusion
  10.4 24.7 %all-gather.6.cloned.1.call-done = bf16[128,4096]{1,0:T(8,128)(2,1)} async-done(((bf16[128,1024]{1,0:T(8,128)(2,1)}), bf16[128,4096]{1,0:T(8,128)(2,1)}) %all-gather.6.cloned.1.call-update) | async-done | bytes 1048592 | tf_op jit(solution)/shard_map/all_gather | solution.py:38
  35.1 94.1 %all-gather.8.cloned.1.call-done = bf16[4096,3,1024]{2,0,1:T(8,128)(2,1)} async-done(((bf16[128,3,1024]{2,0,1:T(8,128)(2,1)}), bf16[4096,3,1024]{2,0,1:T(8,128)(2,1)}) %all-gather.8.cloned.1.call-update) | async-done | bytes 25165840 | tf_op jit(solution)/shard_map/all_gather | solution.py:39
  129.2 5.0 %fusion.27 = bf16[1,128,1024]{2,1,0:T(8,128)(2,1)S(1)} fusion(bf16[128,4096]{1,0:T(8,128)(2,1)} %all-gather.6.cloned.1.call-done, bf16[4096,3,1024]{2,0,1:T(8,128)(2,1)} %all-gather.8.cloned.1.call-done), kind=kOutput, calls=%fused_computation.36 | convolution fusion | flops 1073872896 | bytes 9699328 | tf_op jit(solution)/shard_map/dot_general | solution.py:41
  134.1 4.6 %fusion.28 = bf16[1,128,1024]{2,1,0:T(8,128)(2,1)S(1)} fusion(bf16[128,4096]{1,0:T(8,128)(2,1)S(1)} %copy-done.15, bf16[4096,3,1024]{2,0,1:T(8,128)(2,1)} %all-gather.8.cloned.1.call-done), kind=kOutput, calls=%fused_computation.37 | convolution fusion | flops 1073872896 | bytes 9699328 | tf_op jit(solution)/shard_map/dot_general | solution.py:41
  138.8 4.7 %fusion.29 = bf16[1,128,1024]{2,1,0:T(8,128)(2,1)S(1)} fusion(bf16[128,4096]{1,0:T(8,128)(2,1)S(1)} %copy-done.15, bf16[4096,3,1024]{2,0,1:T(8,128)(2,1)} %all-gather.8.cloned.1.call-done), kind=kOutput, calls=%fused_computation.38 | convolution fusion | flops 1073872896 | bytes 9699328 | tf_op jit(solution)/shard_map/dot_general | solution.py:41
  143.5 2.4 collective-permute-start
  146.1 4.6 %collective-permute-done = bf16[3,2,1024]{2,1,0:T(2,128)(2,1)S(1)} collective-permute-done((bf16[3,2,1024]{2,1,0:T(2,128)(2,1)S(1)}, bf16[3,2,1024]{2,1,0:T(2,128)(2,1)S(1)}, u32[]{:S(2)}, u32[]{:S(2)}) %collective-permute-start) | collective-permute-done | bytes 12320 | tf_op jit(solution)/shard_map/ppermute | solution.py:11
  151.6 1.1 copy-done
  153.5 14.8 %fusion.10 = f32[1024,4,16]{2,1,0:T(4,128)} fusion(f32[4,32,1024]{1,0,2:T(4,128)S(1)} %copy.65, f32[32]{0:T(128)S(1)} %iota_subtract_fusion, f32[16,1024]{0,1:T(8,128)S(1)} %copy.62), kind=kOutput, calls=%fused_computation.16 | convolution fusion | flops 25690112 | bytes 852096 | tf_op jit(solution)/shard_map/spc,bsc->bpc/dot_general | solution.py:64
  168.4 1.9 copy.67
  171.1 1.0 copy.61
  172.2 15.3 %multiply_reduce_fusion = f32[32,1024]{0,1:T(8,128)S(1)} fusion(f32[16,1024]{0,1:T(8,128)S(1)} %copy.62, f32[16,1024]{0,1:T(8,128)} %copy.61), kind=kLoop, calls=%fused_computation.20 | loop fusion | flops 1540096 | bytes 262144 | tf_op jit(solution)/shard_map/reduce_sum | solution.py:58
  187.7 5.4 %gather_fusion = f32[1024,1024]{1,0:T(8,128)} fusion(f32[32,1024]{1,0:T(8,128)S(1)} %copy.63, s32[1024]{0:T(1024)S(1)} %broadcast_clamp_fusion), kind=kCustom, calls=%fused_computation | custom fusion | bytes 8392704 | tf_op jit(solution)/shard_map/gather | solution.py:60
  193.2 14.4 %copy.64 = f32[32,32,1024]{1,0,2:T(8,128)} copy(f32[32,32,1024]{2,1,0:T(8,128)} %bitcast.79) | data formatting | bytes 8388608 | tf_op jit(solution)/shard_map/gather | solution.py:60
  208.4 29.5 %fusion.1 = f32[1024,4,32]{2,1,0:T(4,128)} fusion(f32[4,32,1024]{1,0,2:T(4,128)S(1)} %copy.65, f32[32,32,1024]{1,0,2:T(8,128)} %copy.64, pred[32,32]{1,0:T(8,128)(4,1)S(1)} %subtract_compare_fusion), kind=kOutput, calls=%fused_computation.4 | convolution fusion | flops 51380224 | bytes 5243904 | tf_op jit(solution)/shard_map/tsc,bsc->btc/dot_general | solution.py:62
  238.0 30.1 %while.14 = (s32[]{:T(128)}, f32[16,1024]{1,0:T(8,128)S(1)}, s32[]{:T(128)}, f32[32,16,1024]{2,1,0:T(8,128)}, f32[32,16,1024]{2,1,0:T(8,128)}, /*index=5*/s32[]{:T(128)}, s32[]{:T(128)}) while((s32[]{:T(128)}, f32[16,1024]{1,0:T(8,128)S(1)}, s32[]{:T(128)}, f32[32,16,1024]{2,1,0:T(8,128)}, f32[32,16,1024]{2,1,0:T(8,128)}, ...), condition=%wide.region_2.3_spmd.clone, body=%wide.region_1.2_spmd.clone.sunk | while | flops 65540 | bytes 262253 | solution.py:28
  238.0 1.1 fusion.45
  243.8 0.9 fusion.45
  244.7 0.9 fusion.45
  268.1 1.0 multiply_add_fusion
  269.2 1.7 copy.68
  270.9 12.9 %add_bitcast_fusion = f32[4,32,1024]{1,0,2:T(4,128)} fusion(f32[1024,4,32]{2,1,0:T(4,128)S(1)} %copy-done.2, f32[4,16,1024]{1,0,2:T(4,128)} %copy.68, f32[32]{0:T(128)S(1)} %iota_add_fusion, f32[16,1024]{0,1:T(8,128)S(1)} %copy.62, f32[16,1024]{0,1:T(8,128)S(1)} %copy-done.3), kind=kOutput, calls=%fused_computation.27 | convolution fusion | flops 26345472 | bytes 1441920 | tf_op jit(solution)/shard_map/tpc,bpc->btc/dot_general | solution.py:76
  283.8 2.0 copy.69
  (98 shorter events, 33.7 us)
Async XLA Ops:
  6.5 28.5 %all-gather.6.cloned.1.call-start = ((), (), s32[]{:S(2)}) async-start(), calls=%async_computation | async-start | bytes 1310720 | tf_op jit(solution)/shard_map/all_gather | solution.py:38
  7.3 121.9 %all-gather.8.cloned.1.call-start = ((), (), s32[]{:S(2)}) async-start(), calls=%async_computation.1 | async-start | bytes 25952256 | tf_op jit(solution)/shard_map/all_gather | solution.py:39
  8.0 230.0 %all-gather.12.cloned.1.call-start = ((), (), s32[]{:S(2)}) async-start(), calls=%async_computation.3 | async-start | bytes 2162688 | tf_op jit(solution)/shard_map/all_gather | solution.py:16
  9.5 136.3 %copy-start.11 = (f32[16,1024]{1,0:T(8,128)}, f32[16,1024]{1,0:T(8,128)S(1)}, u32[]{:S(2)}) copy-start(f32[16,1024]{1,0:T(8,128)S(1)} %get-tuple-element.144) | copy-start | bytes 196612
  9.6 228.4 %all-gather.10.cloned.1.call-start = ((), (), s32[]{:S(2)}) async-start(), calls=%async_computation.2 | async-start | bytes 2162688 | tf_op jit(solution)/shard_map/all_gather | solution.py:16
  35.1 99.1 %copy-start.15 = (bf16[128,4096]{1,0:T(8,128)(2,1)S(1)}, bf16[128,4096]{1,0:T(8,128)(2,1)}, u32[]{:S(2)}) copy-start(bf16[128,4096]{1,0:T(8,128)(2,1)} %all-gather.6.cloned.1.call-done) | copy-start | bytes 3145732
  143.5 7.2 %collective-permute-start = (bf16[3,2,1024]{2,1,0:T(2,128)(2,1)S(1)}, bf16[3,2,1024]{2,1,0:T(2,128)(2,1)S(1)}, u32[]{:S(2)}, u32[]{:S(2)}) collective-permute-start(bf16[3,2,1024]{2,1,0:T(2,128)(2,1)S(1)} %pad_maximum_fusion.1), channel_id=1, source_target_pairs={{0,4},{4,8},{8,12},{12,16},{16,20},{20,24},{24,28},{28,32},{32,36}... | collective-permute-start | bytes 36872 | tf_op jit(solution)/shard_map/ppermute | solution.py:11
  151.6 1.1 copy-start
  168.4 1.9 copy-start.6
  168.4 2.7 copy-start.13
  170.3 0.8 copy-start.4
  170.4 0.7 copy-start.7
  170.4 0.8 copy-start.9
  193.1 14.5 %copy-start.5 = (f32[1024,4,16]{0,2,1:T(8,128)S(1)}, f32[1024,4,16]{0,2,1:T(8,128)}, u32[]{:S(2)}) copy-start(f32[1024,4,16]{0,2,1:T(8,128)} %copy-done.4) | copy-start | bytes 786436
  193.1 14.5 %copy-start.8 = (f32[1,16,1024]{2,1,0:T(8,128)S(1)}, f32[1,16,1024]{2,1,0:T(8,128)}, u32[]{:S(2)}) copy-start(f32[1,16,1024]{2,1,0:T(8,128)} %copy-done.7) | copy-start | bytes 196612
  193.1 14.5 %copy-start.10 = (f32[1,16,1024]{2,1,0:T(8,128)S(1)}, f32[1,16,1024]{2,1,0:T(8,128)}, u32[]{:S(2)}) copy-start(f32[1,16,1024]{2,1,0:T(8,128)} %copy-done.9) | copy-start | bytes 196612
  208.4 59.7 %copy-start.12 = (f32[16,1024]{1,0:T(8,128)S(1)}, f32[16,1024]{1,0:T(8,128)}, u32[]{:S(2)}) copy-start(f32[16,1024]{1,0:T(8,128)} %copy-done.11) | copy-start | bytes 196612
  238.0 32.9 %copy-start.2 = (f32[1024,4,32]{2,1,0:T(4,128)S(1)}, f32[1024,4,32]{2,1,0:T(4,128)}, u32[]{:S(2)}) copy-start(f32[1024,4,32]{2,1,0:T(4,128)} %fusion.1) | copy-start | bytes 1572868
  238.0 32.9 %copy-start.3 = (f32[16,1024]{0,1:T(8,128)S(1)}, f32[16,1024]{0,1:T(8,128)}, u32[]{:S(2)}) copy-start(f32[16,1024]{0,1:T(8,128)} %copy.61) | copy-start | bytes 196612
  283.8 2.0 copy-start.1
  283.8 2.0 copy-start.14
Sparse Core Ops, SparseCore 0:
  9.0 25.9 all-gather.5
  37.4 91.7 all-gather.7
  131.4 43.6 all-gather.11
  177.3 43.2 all-gather.9
where the time goes:
time: 295 us; the launch traced here: 293 us
  waiting for transfers between devices  125 us (42%)
  matrix products  71.5 us (24%)
  other arithmetic  49.9 us (17%)
  local copies, waits for them, and re-layouts  30.4 us (10%)
  between operations  13.5 us (5%)
    all_gather x1, waiting for transfers between devices, per_device(): piece = lax.all_gather(in_weight, 'ctx', axis=0, tiled=True)  94.1 us
    dot_general x1, matrix products, per_device(): jnp.einsum('tsc,bsc->btc', toeplitz, blocked, precision=lax.Precision.HIG...  29.5 us
    select_n x32, other arithmetic, turn(): return jax.tree.map(lambda a, b: jnp.where(reached, a, b), new, before)  29.4 us
    all_gather x1, waiting for transfers between devices, per_device(): whole = lax.all_gather(tokens, 'tp', axis=1, tiled=True)  24.7 us
    gather x2, local copies, waits for them, and re-layouts, per_device(): response[jnp.clip(lags, 0, span - 1)]  19.8 us
    reduce_sum x1, other arithmetic, per_device(): response = jnp.sum(residue[None] * powers, axis=1)  15.3 us
    dot_general x1, matrix products, per_device(): jnp.einsum('spc,bsc->bpc', tails, blocked, precision=lax.Precision.HIGHEST)  14.8 us
    dot_general x3, matrix products, per_device(): jnp.dot(whole, piece[:, g, :], preferred_element_type=jnp.float32)  14.3 us
  transfers between devices with their start and end apart: 5, of which 3 were waited for; matrix products, arithmetic and copies ran while one was open for 35% of the time, Pallas kernels for 0%

commit v1 on v0

--- a/solution.py
+++ b/solution.py
@@ -35,7 +35,9 @@
 def per_device(tokens, in_weight, conv_taps, decay_rate, residue, skip):
     rows = tokens.shape[0]
     chans = in_weight.shape[2]
-    whole = lax.all_gather(tokens, "tp", axis=1, tiled=True)
+    whole = jnp.concatenate(
+        lax.all_to_all(jnp.stack([tokens] * lax.axis_size("tp")), "tp", 0, 0), axis=1
+    )
     piece = lax.all_gather(in_weight, "ctx", axis=0, tiled=True)
     sums = tuple(
         (jnp.dot(whole, piece[:, g, :], preferred_element_type=jnp.float32) for g in range(3))

time: 295 us -> 269 us (0.912)
  waiting for transfers between devices: 125 us -> 93.6 us
  starting transfers between devices: 2.47 us -> 6.87 us
    all_gather x1 -> x0, waiting for transfers between devices: 24.7 us -> none  [per_device(): whole = lax.all_gather(tokens, 'tp', axis=1, tiled=True)]
    all_gather x1, waiting for transfers between devices: 94.1 us -> 74.1 us  [per_device(): piece = lax.all_gather(in_weight, 'ctx', axis=0, tiled=True)]
    all_to_all x0 -> x1, waiting for transfers between devices: none -> 14.3 us  [per_device(): lax.all_to_all(jnp.stack([tokens] * lax.axis_size('tp')), 'tp', 0, 0)]
    all_to_all x0 -> x1, starting transfers between devices: none -> 4.46 us  [per_device(): lax.all_to_all(jnp.stack([tokens] * lax.axis_size('tp')), 'tp', 0, 0)]
  transfers between devices with their start and end apart: 5 -> 5, of which waited for: 3 -> 3; matrix products, arithmetic and copies ran while one was open for 35% -> 39% of each run, Pallas kernels for 0% -> 0%
where the time goes in v1:
time: 269 us; the launch traced here: 267 us
  waiting for transfers between devices  93.6 us (35%)
  matrix products  71.3 us (27%)
  other arithmetic  49.1 us (18%)
  local copies, waits for them, and re-layouts  32 us (12%)
  between operations  13.5 us (5%)
  starting transfers between devices  6.87 us (3%)
    all_gather x1, waiting for transfers between devices, per_device(): piece = lax.all_gather(in_weight, 'ctx', axis=0, tiled=True)  74.1 us
    dot_general x1, matrix products, per_device(): jnp.einsum('tsc,bsc->btc', toeplitz, blocked, precision=lax.Precision.HIG...  29.5 us
    select_n x32, other arithmetic, turn(): return jax.tree.map(lambda a, b: jnp.where(reached, a, b), new, before)  29.4 us
    gather x2, local copies, waits for them, and re-layouts, per_device(): response[jnp.clip(lags, 0, span - 1)]  19.9 us
    reduce_sum x1, other arithmetic, per_device(): response = jnp.sum(residue[None] * powers, axis=1)  15.3 us
    dot_general x1, matrix products, per_device(): jnp.einsum('spc,bsc->bpc', tails, blocked, precision=lax.Precision.HIGHEST)  14.8 us
    all_to_all x1, waiting for transfers between devices, per_device(): lax.all_to_all(jnp.stack([tokens] * lax.axis_size('tp')), 'tp', 0, 0)  14.3 us
    dot_general x3, matrix products, per_device(): jnp.dot(whole, piece[:, g, :], preferred_element_type=jnp.float32)  14 us
  transfers between devices with their start and end apart: 5, of which 3 were waited for; matrix products, arithmetic and copies ran while one was open for 39% of the time, Pallas kernels for 0%

profile of v1, /device:TPU:32, one launch (start us, length us, event | category | flops | bytes accessed | tf_op | source)
XLA Modules:
  0.0 267.0 jit_solution(7396639220630744042)
XLA Ops:
  7.3 1.1 copy.64
  8.4 1.1 stack.19
  9.6 4.5 %all-to-all-start = ((bf16[4,128,1024]{1,2,0:T(8,128)(2,1)}), bf16[4,128,1024]{1,2,0:T(8,128)(2,1)S(1)}, u32[]{:S(2)}, u32[]{:S(2)}) async-start(bf16[4,128,1024]{1,2,0:T(8,128)(2,1)} %stack.19), calls=%async_computation | async-start | bytes 2097152 | tf_op jit(solution)/shard_map/all_to_all | solution.py:39
  14.8 14.3 %all-to-all-done = bf16[4,128,1024]{1,2,0:T(8,128)(2,1)S(1)} async-done(((bf16[4,128,1024]{1,2,0:T(8,128)(2,1)}), bf16[4,128,1024]{1,2,0:T(8,128)(2,1)S(1)}, u32[]{:S(2)}, u32[]{:S(2)}) %all-to-all-start) | async-done | bytes 1048608 | tf_op jit(solution)/shard_map/all_to_all | solution.py:39
  29.1 74.1 %all-gather.5.cloned.1.call-done = bf16[4096,3,1024]{2,0,1:T(8,128)(2,1)} async-done(((bf16[128,3,1024]{2,0,1:T(8,128)(2,1)}), bf16[4096,3,1024]{2,0,1:T(8,128)(2,1)}) %all-gather.5.cloned.1.call-update) | async-done | bytes 25165840 | tf_op jit(solution)/shard_map/all_gather | solution.py:41
  103.2 4.7 %fusion.27 = bf16[1,128,1024]{2,1,0:T(8,128)(2,1)S(1)} fusion(bf16[128,4096]{0,1:T(8,128)(2,1)S(1)} %bitcast.86, bf16[4096,3,1024]{2,0,1:T(8,128)(2,1)} %all-gather.5.cloned.1.call-done), kind=kOutput, calls=%fused_computation.36 | convolution fusion | flops 1073872896 | bytes 9699328 | tf_op jit(solution)/shard_map/dot_general | solution.py:43
  107.8 4.7 %fusion.28 = bf16[1,128,1024]{2,1,0:T(8,128)(2,1)S(1)} fusion(bf16[128,4096]{0,1:T(8,128)(2,1)S(1)} %bitcast.87, bf16[4096,3,1024]{2,0,1:T(8,128)(2,1)} %all-gather.5.cloned.1.call-done), kind=kOutput, calls=%fused_computation.37 | convolution fusion | flops 1073872896 | bytes 9699328 | tf_op jit(solution)/shard_map/dot_general | solution.py:43
  112.5 4.7 %fusion.29 = bf16[1,128,1024]{2,1,0:T(8,128)(2,1)S(1)} fusion(bf16[128,4096]{0,1:T(8,128)(2,1)S(1)} %bitcast.88, bf16[4096,3,1024]{2,0,1:T(8,128)(2,1)} %all-gather.5.cloned.1.call-done), kind=kOutput, calls=%fused_computation.38 | convolution fusion | flops 1073872896 | bytes 9699328 | tf_op jit(solution)/shard_map/dot_general | solution.py:43
  117.2 2.4 collective-permute-start
  119.8 4.5 %collective-permute-done = bf16[3,2,1024]{2,1,0:T(2,128)(2,1)S(1)} collective-permute-done((bf16[3,2,1024]{2,1,0:T(2,128)(2,1)S(1)}, bf16[3,2,1024]{2,1,0:T(2,128)(2,1)S(1)}, u32[]{:S(2)}, u32[]{:S(2)}) %collective-permute-start) | collective-permute-done | bytes 12320 | tf_op jit(solution)/shard_map/ppermute | solution.py:11
  125.3 1.1 copy-done
  127.2 14.8 %fusion.10 = f32[1024,4,16]{2,1,0:T(4,128)} fusion(f32[4,32,1024]{1,0,2:T(4,128)S(1)} %copy.69, f32[32]{0:T(128)S(1)} %iota_subtract_fusion, f32[16,1024]{0,1:T(8,128)S(1)} %copy.66), kind=kOutput, calls=%fused_computation.16 | convolution fusion | flops 25690112 | bytes 852096 | tf_op jit(solution)/shard_map/spc,bsc->bpc/dot_general | solution.py:66
  142.1 1.9 copy.71
  144.8 1.0 copy.65
  145.9 15.3 %multiply_reduce_fusion = f32[32,1024]{0,1:T(8,128)S(1)} fusion(f32[16,1024]{0,1:T(8,128)S(1)} %copy.66, f32[16,1024]{0,1:T(8,128)} %copy.65), kind=kLoop, calls=%fused_computation.20 | loop fusion | flops 1540096 | bytes 262144 | tf_op jit(solution)/shard_map/reduce_sum | solution.py:60
  161.4 5.5 %gather_fusion = f32[1024,1024]{1,0:T(8,128)} fusion(f32[32,1024]{1,0:T(8,128)S(1)} %copy.67, s32[1024]{0:T(1024)S(1)} %broadcast_clamp_fusion), kind=kCustom, calls=%fused_computation | custom fusion | bytes 8392704 | tf_op jit(solution)/shard_map/gather | solution.py:62
  166.9 14.4 %copy.68 = f32[32,32,1024]{1,0,2:T(8,128)} copy(f32[32,32,1024]{2,1,0:T(8,128)} %bitcast.82) | data formatting | bytes 8388608 | tf_op jit(solution)/shard_map/gather | solution.py:62
  182.2 29.5 %fusion.1 = f32[1024,4,32]{2,1,0:T(4,128)} fusion(f32[4,32,1024]{1,0,2:T(4,128)S(1)} %copy.69, f32[32,32,1024]{1,0,2:T(8,128)} %copy.68, pred[32,32]{1,0:T(8,128)(4,1)S(1)} %subtract_compare_fusion), kind=kOutput, calls=%fused_computation.4 | convolution fusion | flops 51380224 | bytes 5243904 | tf_op jit(solution)/shard_map/tsc,bsc->btc/dot_general | solution.py:64
  211.7 30.1 %while.14 = (s32[]{:T(128)}, f32[16,1024]{1,0:T(8,128)S(1)}, s32[]{:T(128)}, f32[32,16,1024]{2,1,0:T(8,128)}, f32[32,16,1024]{2,1,0:T(8,128)}, /*index=5*/s32[]{:T(128)}, s32[]{:T(128)}) while((s32[]{:T(128)}, f32[16,1024]{1,0:T(8,128)S(1)}, s32[]{:T(128)}, f32[32,16,1024]{2,1,0:T(8,128)}, f32[32,16,1024]{2,1,0:T(8,128)}, ...), condition=%wide.region_2.3_spmd.clone, body=%wide.region_1.2_spmd.clone.sunk | while | flops 65540 | bytes 262253 | solution.py:28
  211.8 1.1 fusion.45
  241.9 1.0 multiply_add_fusion
  242.9 1.7 copy.72
  244.7 12.9 %add_bitcast_fusion = f32[4,32,1024]{1,0,2:T(4,128)} fusion(f32[1024,4,32]{2,1,0:T(4,128)S(1)} %copy-done.2, f32[4,16,1024]{1,0,2:T(4,128)} %copy.72, f32[32]{0:T(128)S(1)} %iota_add_fusion, f32[16,1024]{0,1:T(8,128)S(1)} %copy.66, f32[16,1024]{0,1:T(8,128)S(1)} %copy-done.3), kind=kOutput, calls=%fused_computation.27 | convolution fusion | flops 26345472 | bytes 1441920 | tf_op jit(solution)/shard_map/tpc,bpc->btc/dot_general | solution.py:78
  257.5 2.0 copy.73
  (99 shorter events, 34.7 us)
Async XLA Ops:
  6.5 96.6 %all-gather.5.cloned.1.call-start = ((), (), s32[]{:S(2)}) async-start(), calls=%async_computation.1 | async-start | bytes 25952256 | tf_op jit(solution)/shard_map/all_gather | solution.py:41
  7.3 6.8 %copy-start.6 = (f32[16,1024]{1,0:T(8,128)S(1)}, f32[16,1024]{1,0:T(8,128)}, u32[]{:S(2)}) copy-start(f32[16,1024]{1,0:T(8,128)} %param.11) | copy-start | bytes 196612
  7.3 7.5 %copy-start.14 = (f32[3,3,1024]{2,1,0:T(4,128)S(1)}, f32[3,3,1024]{2,1,0:T(4,128)}, u32[]{:S(2)}) copy-start(f32[3,3,1024]{2,1,0:T(4,128)} %param.10) | copy-start | bytes 110596
  9.6 19.6 %all-to-all-start = ((bf16[4,128,1024]{1,2,0:T(8,128)(2,1)}), bf16[4,128,1024]{1,2,0:T(8,128)(2,1)S(1)}, u32[]{:S(2)}, u32[]{:S(2)}) async-start(bf16[4,128,1024]{1,2,0:T(8,128)(2,1)} %stack.19), calls=%async_computation | async-start | bytes 2097152 | tf_op jit(solution)/shard_map/all_to_all | solution.py:39
  14.0 197.7 %all-gather.9.cloned.1.call-start = ((), (), s32[]{:S(2)}) async-start(), calls=%async_computation.3 | async-start | bytes 2162688 | tf_op jit(solution)/shard_map/all_gather | solution.py:16
  14.7 104.9 %copy-start.11 = (f32[16,1024]{1,0:T(8,128)}, f32[16,1024]{1,0:T(8,128)S(1)}, u32[]{:S(2)}) copy-start(f32[16,1024]{1,0:T(8,128)S(1)} %get-tuple-element.144) | copy-start | bytes 196612
  14.8 197.0 %all-gather.7.cloned.1.call-start = ((), (), s32[]{:S(2)}) async-start(), calls=%async_computation.2 | async-start | bytes 2162688 | tf_op jit(solution)/shard_map/all_gather | solution.py:16
  117.2 7.1 %collective-permute-start = (bf16[3,2,1024]{2,1,0:T(2,128)(2,1)S(1)}, bf16[3,2,1024]{2,1,0:T(2,128)(2,1)S(1)}, u32[]{:S(2)}, u32[]{:S(2)}) collective-permute-start(bf16[3,2,1024]{2,1,0:T(2,128)(2,1)S(1)} %pad_maximum_fusion.1), channel_id=1, source_target_pairs={{0,4},{4,8},{8,12},{12,16},{16,20},{20,24},{24,28},{28,32},{32,36}... | collective-permute-start | bytes 36872 | tf_op jit(solution)/shard_map/ppermute | solution.py:11
  125.2 1.1 copy-start
  142.1 2.8 %copy-start.13 = (f32[16,1024]{1,0:T(8,128)S(1)}, f32[16,1024]{1,0:T(8,128)}, u32[]{:S(2)}) copy-start(f32[16,1024]{1,0:T(8,128)} %param.12) | copy-start | bytes 196612
  144.0 0.8 copy-start.4
  144.1 0.8 copy-start.7
  144.1 0.8 copy-start.9
  166.9 14.5 %copy-start.5 = (f32[1024,4,16]{0,2,1:T(8,128)S(1)}, f32[1024,4,16]{0,2,1:T(8,128)}, u32[]{:S(2)}) copy-start(f32[1024,4,16]{0,2,1:T(8,128)} %copy-done.4) | copy-start | bytes 786436
  166.9 14.5 %copy-start.8 = (f32[1,16,1024]{2,1,0:T(8,128)S(1)}, f32[1,16,1024]{2,1,0:T(8,128)}, u32[]{:S(2)}) copy-start(f32[1,16,1024]{2,1,0:T(8,128)} %copy-done.7) | copy-start | bytes 196612
  166.9 14.5 %copy-start.10 = (f32[1,16,1024]{2,1,0:T(8,128)S(1)}, f32[1,16,1024]{2,1,0:T(8,128)}, u32[]{:S(2)}) copy-start(f32[1,16,1024]{2,1,0:T(8,128)} %copy-done.9) | copy-start | bytes 196612
  182.2 59.7 %copy-start.12 = (f32[16,1024]{1,0:T(8,128)S(1)}, f32[16,1024]{1,0:T(8,128)}, u32[]{:S(2)}) copy-start(f32[16,1024]{1,0:T(8,128)} %copy-done.11) | copy-start | bytes 196612
  211.7 32.9 %copy-start.2 = (f32[1024,4,32]{2,1,0:T(4,128)S(1)}, f32[1024,4,32]{2,1,0:T(4,128)}, u32[]{:S(2)}) copy-start(f32[1024,4,32]{2,1,0:T(4,128)} %fusion.1) | copy-start | bytes 1572868
  211.7 32.9 %copy-start.3 = (f32[16,1024]{0,1:T(8,128)S(1)}, f32[16,1024]{0,1:T(8,128)}, u32[]{:S(2)}) copy-start(f32[16,1024]{0,1:T(8,128)} %copy.65) | copy-start | bytes 196612
  257.5 2.0 copy-start.1
  257.5 2.0 copy-start.15
Sparse Core Ops, SparseCore 0:
  9.7 93.4 all-gather.4
  105.4 43.6 all-gather.8
  151.4 43.2 all-gather.6
